TPU v7x, 32 devices: a whole 2x2x4 slice. The times are simulated.
32 devices in a mesh: groups: 2 (over y), seq: 4 (over z), head: 2 (over x), sub: 2 (over core).
Axes of the slice: x: 2, y: 2, z: 4, core: 2. Of those that a mesh axis runs over, the one named last changes fastest.
Arguments:
- hidden_states: bfloat16 [8192, 8192], P(('groups', 'seq', 'sub'), 'head'), parts along dimension 0, may hold values from -42 to 42
- key_projection_weight: bfloat16 [8192, 1024], P(('seq', 'sub'), 'head'), may hold values from -0.0625 to 0.0625
- value_projection_weight: bfloat16 [8192, 1024], P(('seq', 'sub'), 'head'), may hold values from -0.0625 to 0.0625
- head_basis_matrix: float32 [8, 128, 64], P('head'), may hold values from -0.5 to 0.5
- slot_token: int32 [8192], P(('groups', 'seq', 'sub')), parts along dimension 0, may hold values from 0 to 4095, as said below
Outputs:
- compressed_keys: bfloat16 [8192, 512], P(('groups', 'seq', 'sub'), 'head'), parts along dimension 0
- value_cache: bfloat16 [8192, 1024], P(('groups', 'seq', 'sub'), 'head'), parts along dimension 0
There are 2 independent parts, one for each index of `groups`. A program takes and returns all parts, laid end to end along the dimension named above; an argument that names none is the same for every part. Nothing has to cross between parts.
Inputs may be any that keep to these rules, and one draw needn't show every extreme that they name: `slot_token`: A permutation of the 4096 token positions. Each aligned block of 512 rows holds exactly 64 positions of each aligned block of 512 positions.
All inputs are finite; a program needn't handle non-finite values.
Results may differ from a plain program's by a relative error of at most 0.0055.
Values may be sent and summed in bfloat16 or wider, within the bound.
No kernel may reach another device: no remote copies, remote signals or barrier semaphores. Data moves between devices by JAX's collectives and lax.ppermute only.
A program may use at most 64 MiB of HBM per device.

v0:
```python
import jax
import jax.numpy as jnp
from jax import lax
from jax.sharding import PartitionSpec as P

ridge_share = 0.05


def covariance_sum(decode_key_cache, heads_here, head_dim, token_total):
    per_head_keys = decode_key_cache.reshape(decode_key_cache.shape[0], heads_here, head_dim)
    local_terms = jnp.einsum(
        "thi,thj->hij", per_head_keys, per_head_keys, preferred_element_type=jnp.float32
    )
    summed = lax.psum(local_terms, ("seq", "sub"))
    return summed / token_total


def per_device(
    hidden_states, key_projection_weight, value_projection_weight, head_basis_matrix, slot_token
):
    tokens_here = hidden_states.shape[0]
    seq_count = lax.axis_size("seq")
    core_count = lax.axis_size("sub")
    device_count = seq_count * core_count
    token_total = tokens_here * device_count
    heads_here = head_basis_matrix.shape[0]
    head_dim = head_basis_matrix.shape[1]
    rank_dim = head_basis_matrix.shape[2]
    gathered = lax.all_gather(hidden_states, "head", axis=1, tiled=True)
    key_sums = jnp.dot(
        gathered,
        lax.all_gather(key_projection_weight, ("seq", "sub"), axis=0, tiled=True),
        preferred_element_type=jnp.float32,
    )
    value_sums = jnp.dot(
        gathered,
        lax.all_gather(value_projection_weight, ("seq", "sub"), axis=0, tiled=True),
        preferred_element_type=jnp.float32,
    )
    decode_key_cache = key_sums.astype(jnp.bfloat16)
    moments = covariance_sum(decode_key_cache, heads_here, head_dim, token_total)
    value_cache = value_sums.astype(jnp.bfloat16)
    trace_vals = jnp.trace(moments, axis1=1, axis2=2)
    identity = jnp.eye(head_dim, dtype=jnp.float32)
    regular = moments + (ridge_share * trace_vals / head_dim)[:, None, None] * identity
    factor = jnp.linalg.cholesky(regular)
    by_head = jnp.transpose(
        decode_key_cache.astype(jnp.float32).reshape(tokens_here, heads_here, head_dim), (1, 0, 2)
    )
    whitened = lax.linalg.triangular_solve(
        factor, by_head, left_side=False, lower=True, transpose_a=True
    )
    basis_coefficients = jnp.einsum(
        "htd,hdr->htr", whitened, head_basis_matrix, precision=lax.Precision.HIGHEST
    )
    compressed = (
        jnp.transpose(basis_coefficients, (1, 0, 2))
        .reshape(tokens_here, heads_here * rank_dim)
        .astype(jnp.bfloat16)
    )
    row_order = jnp.argsort(slot_token)
    wanted = slot_token[row_order]
    asked = lax.all_to_all(wanted, ("seq", "sub"), split_axis=0, concat_axis=0, tiled=True)
    local_rows = asked % tokens_here
    got_coeffs, got_values = (
        lax.all_to_all(
            compressed[local_rows], ("seq", "sub"), split_axis=0, concat_axis=0, tiled=True
        ),
        lax.all_to_all(
            value_cache[local_rows], ("seq", "sub"), split_axis=0, concat_axis=0, tiled=True
        ),
    )
    inverse = jnp.argsort(row_order)
    return (got_coeffs[inverse], got_values[inverse])


def solution(mesh):
    return jax.shard_map(
        per_device,
        mesh=mesh,
        in_specs=(
            P(("groups", "seq", "sub"), "head"),
            P(("seq", "sub"), "head"),
            P(("seq", "sub"), "head"),
            P("head", None, None),
            P(("groups", "seq", "sub")),
        ),
        out_specs=(P(("groups", "seq", "sub"), "head"), P(("groups", "seq", "sub"), "head")),
        check_vma=False,
    )
```

profile of v0, /device:TPU:0, one launch (start us, length us, event | category | flops | bytes accessed | tf_op | source)
XLA Modules:
  0.0 405.3 jit_solution(3034889648175689121)
XLA Ops:
  7.2 0.7 all-gather.4.cloned.1.call-update
  8.0 0.7 all-gather.6.cloned.1.call-update
  8.7 107.6 %all-gather.4.cloned.1.call-done = bf16[512,8192]{1,0:T(8,128)(2,1)} async-done(((bf16[512,4096]{1,0:T(8,128)(2,1)}), bf16[512,8192]{1,0:T(8,128)(2,1)}) %all-gather.4.cloned.1.call-update) | async-done | bytes 8388624 | tf_op jit(solution)/shard_map/all_gather | solution.py:29
  116.3 83.7 %all-gather.6.cloned.1.call-done = bf16[8192,512]{1,0:T(8,128)(2,1)} async-done(((bf16[1024,512]{1,0:T(8,128)(2,1)}), bf16[8192,512]{1,0:T(8,128)(2,1)}) %all-gather.6.cloned.1.call-update) | async-done | bytes 8388624 | tf_op jit(solution)/shard_map/all_gather | solution.py:32
  200.0 10.3 %convolution_convert_fusion.1 = bf16[512,512]{0,1:T(8,128)(2,1)S(1)} fusion(bf16[512,8192]{1,0:T(8,128)(2,1)} %all-gather.4.cloned.1.call-done, bf16[8192,512]{1,0:T(8,128)(2,1)} %all-gather.6.cloned.1.call-done), kind=kOutput, calls=%fused_computation.6 | convolution fusion | flops 4295229440 | bytes 17301504 | tf_op jit(solution)/shard_map/dot_general | solution.py:30
  210.3 1.0 fusion.6
  211.4 0.5 all-gather.8.cloned.1.call-update
  211.9 3.8 sort.31
  215.7 3.5 gather_fusion
  219.2 0.7 all_to_all.24
  219.9 3.5 all-to-all-start
  223.4 5.2 %all-to-all-done = s32[8,64,1]{1,2,0:T(1,128)S(1)} async-done(((s32[8,64,1]{1,2,0:T(1,128)}), s32[8,64,1]{1,2,0:T(1,128)S(1)}, u32[]{:S(2)}, u32[]{:S(2)}) %all-to-all-start) | async-done | bytes 2080 | tf_op jit(solution)/shard_map/all_to_all | solution.py:63
  228.6 0.5 broadcast.144
  229.1 0.7 reduce.9
  229.9 0.3 copy.19
  230.2 34.9 %all-reduce.2.cloned.1.call-done = f32[4,128,128]{2,1,0:T(8,128)} async-done(((f32[4,128,128]{2,1,0:T(8,128)}), f32[4,128,128]{2,1,0:T(8,128)}) %all-reduce.2.cloned.1.call-update) | async-done | bytes 262160 | tf_op jit(solution)/shard_map/psum | solution.py:14
  265.1 1.1 select_reduce_fusion.1
  266.1 1.0 multiply_add_fusion
  267.3 1.1 fusion.3
  268.4 46.9 %custom-call.7 = f32[4,128,128]{2,1,0:T(8,128)S(1)} custom-call(f32[4,128,128]{2,1,0:T(8,128)S(1)} %fusion.3), custom_call_target="Cholesky" | custom-call | tf_op jit(solution)/shard_map/jit(cholesky)/cholesky | solution.py:46
  315.6 39.3 %custom-call.8 = f32[4,1,128,128]{2,3,1,0:T(8,128)S(1)} custom-call(f32[4,1,128,128]{3,2,1,0:T(8,128)S(1)} %select_bitcast_fusion), custom_call_target="InvertDiagBlocksLowerTriangular" | custom-call | tf_op jit(solution)/shard_map/triangular_solve | solution.py:50
  354.9 0.6 fusion
  355.5 1.3 convolution_convert_fusion.2
  356.9 2.6 gather_fusion.1
  359.5 3.6 all-to-all-start.1
  363.1 10.2 %convolution_convert_fusion = bf16[512,512]{1,0:T(8,128)(2,1)S(1)} fusion(bf16[512,8192]{1,0:T(8,128)(2,1)} %all-gather.4.cloned.1.call-done, bf16[8192,512]{1,0:T(8,128)(2,1)} %all-gather.8.cloned.1.call-done), kind=kOutput, calls=%fused_computation.5 | convolution fusion | flops 4295229440 | bytes 17301504 | tf_op jit(solution)/shard_map/dot_general | solution.py:35
  373.4 2.6 gather_fusion.3
  376.0 4.8 %all-to-all-start.2 = ((bf16[8,64,512]{2,1,0:T(8,128)(2,1)}), bf16[8,64,512]{2,1,0:T(8,128)(2,1)S(1)}, u32[]{:S(2)}, u32[]{:S(2)}) async-start(bf16[8,64,512]{2,1,0:T(8,128)(2,1)} %bitcast.11), calls=%async_computation.2 | async-start | bytes 1048576 | tf_op jit(solution)/shard_map/all_to_all | solution.py:69
  380.8 3.8 sort.32
  384.6 2.6 gather_fusion.2
  387.2 9.0 %all-to-all-done.2 = bf16[8,64,512]{2,1,0:T(8,128)(2,1)S(1)} async-done(((bf16[8,64,512]{2,1,0:T(8,128)(2,1)}), bf16[8,64,512]{2,1,0:T(8,128)(2,1)S(1)}, u32[]{:S(2)}, u32[]{:S(2)}) %all-to-all-start.2) | async-done | bytes 524320 | tf_op jit(solution)/shard_map/all_to_all | solution.py:69
  396.2 2.6 gather_fusion.4
  (29 shorter events, 0.9 us)
Async XLA Ops:
  7.2 348.3 %copy-start = (f32[4,128,64]{1,2,0:T(8,128)S(1)}, f32[4,128,64]{1,2,0:T(8,128)}, u32[]{:S(2)}) copy-start(f32[4,128,64]{1,2,0:T(8,128)} %param.8) | copy-start | bytes 393220
  7.2 109.1 %all-gather.4.cloned.1.call-start = ((), (), s32[]{:S(2)}) async-start(), calls=%async_computation.3 | async-start | bytes 12582912 | tf_op jit(solution)/shard_map/all_gather | solution.py:29
  7.9 192.1 %all-gather.6.cloned.1.call-start = ((), (), s32[]{:S(2)}) async-start(), calls=%async_computation.4 | async-start | bytes 9437184 | tf_op jit(solution)/shard_map/all_gather | solution.py:32
  8.7 203.2 %copy-start.1 = (s32[512]{0:T(512)S(1)}, s32[512]{0:T(512)}, u32[]{:S(2)}) copy-start(s32[512]{0:T(512)} %param.9) | copy-start | bytes 6148
  8.7 256.4 %all-reduce.2.cloned.1.call-start = ((), (), s32[]{:S(2)}) async-start(), calls=%async_computation.5 | async-start | bytes 524288 | tf_op jit(solution)/shard_map/psum | solution.py:14
  211.3 151.8 %all-gather.8.cloned.1.call-start = ((), (), s32[]{:S(2)}) async-start(), calls=%async_computation.6 | async-start | bytes 9437184 | tf_op jit(solution)/shard_map/all_gather | solution.py:37
  219.9 8.7 %all-to-all-start = ((s32[8,64,1]{1,2,0:T(1,128)}), s32[8,64,1]{1,2,0:T(1,128)S(1)}, u32[]{:S(2)}, u32[]{:S(2)}) async-start(s32[8,64,1]{1,2,0:T(1,128)} %bitcast.7), calls=%async_computation | async-start | bytes 8192 | tf_op jit(solution)/shard_map/all_to_all | solution.py:63
  359.5 16.6 %all-to-all-start.1 = ((bf16[8,64,256]{2,1,0:T(8,128)(2,1)}), bf16[8,64,256]{2,1,0:T(8,128)(2,1)S(1)}, u32[]{:S(2)}, u32[]{:S(2)}) async-start(bf16[8,64,256]{2,1,0:T(8,128)(2,1)} %bitcast.9), calls=%async_computation.1 | async-start | bytes 524288 | tf_op jit(solution)/shard_map/all_to_all | solution.py:66
  376.0 20.1 %all-to-all-start.2 = ((bf16[8,64,512]{2,1,0:T(8,128)(2,1)}), bf16[8,64,512]{2,1,0:T(8,128)(2,1)S(1)}, u32[]{:S(2)}, u32[]{:S(2)}) async-start(bf16[8,64,512]{2,1,0:T(8,128)(2,1)} %bitcast.11), calls=%async_computation.2 | async-start | bytes 1048576 | tf_op jit(solution)/shard_map/all_to_all | solution.py:69
Sparse Core Ops, SparseCore 0:
  9.6 106.6 all-gather.3
  117.9 82.0 all-gather.5
  211.4 53.5 all-reduce.1
  266.6 81.1 all-gather.7
where the time goes:
time: 406 us; the launch traced here: 405 us
  waiting for transfers between devices  242 us (60%)
  other arithmetic  98 us (24%)
  matrix products  23.4 us (6%)
  local copies, waits for them, and re-layouts  15.7 us (4%)
  between operations  13.9 us (3%)
  starting transfers between devices  12.1 us (3%)
    all_gather x1, waiting for transfers between devices, per_device(): gathered = lax.all_gather(hidden_states, 'head', axis=1, tiled=True)  108 us
    all_gather x1, waiting for transfers between devices, per_device(): lax.all_gather(key_projection_weight, ('seq', 'sub'), axis=0, tiled=True)  83.7 us
    another operation x4, other arithmetic, per_device(): factor = jnp.linalg.cholesky(regular)  47.1 us
    another operation x3, other arithmetic, per_device(): lax.linalg.triangular_solve(factor, by_head, left_side=False, lower=True,...  39.4 us
    psum x1, waiting for transfers between devices, covariance_sum(): summed = lax.psum(local_terms, ('seq', 'sub'))  34.9 us
    dot_general x1, matrix products, per_device(): jnp.dot(gathered, lax.all_gather(key_projection_weight, ('seq', 'sub'), a...  10.3 us
    dot_general x1, matrix products, per_device(): jnp.dot(gathered, lax.all_gather(value_projection_weight, ('seq', 'sub'),...  10.2 us
    all_to_all x1, waiting for transfers between devices, per_device(): lax.all_to_all(value_cache[local_rows], ('seq', 'sub'), split_axis=0, con...  9 us
  transfers between devices with their start and end apart: 7, of which 5 were waited for; matrix products, arithmetic and copies ran while one was open for 30% of the time, Pallas kernels for 0%

commit v1 on v0

--- a/solution.py
+++ b/solution.py
@@ -11,7 +11,7 @@
     local_terms = jnp.einsum(
         "thi,thj->hij", per_head_keys, per_head_keys, preferred_element_type=jnp.float32
     )
-    summed = lax.psum(local_terms, ("seq", "sub"))
+    summed = jnp.sum(lax.all_gather(local_terms, ("seq", "sub")), axis=0)
     return summed / token_total
 
 

time: 406 us -> 438 us (1.079)
  waiting for transfers between devices: 242 us -> 277 us
    all_gather x1, waiting for transfers between devices: 0.02 us -> 52.6 us  [per_device(): lax.all_gather(value_projection_weight, ('seq', 'sub'), axis=0, tiled=True)]
    psum x1 -> x0, waiting for transfers between devices: 34.9 us -> none  [covariance_sum(): summed = lax.psum(local_terms, ('seq', 'sub'))]
    all_gather x0 -> x1, waiting for transfers between devices: none -> 23.4 us  [covariance_sum(): summed = jnp.sum(lax.all_gather(local_terms, ('seq', 'sub')), axis=0)]
    all_to_all x1, waiting for transfers between devices: 9 us -> 0.01 us  [per_device(): lax.all_to_all(value_cache[local_rows], ('seq', 'sub'), split_axis=0, con...]
  transfers between devices with their start and end apart: 7 -> 7, of which waited for: 5 -> 6; matrix products, arithmetic and copies ran while one was open for 30% -> 30% of each run, Pallas kernels for 0% -> 0%
where the time goes in v1:
time: 438 us
  waiting for transfers between devices  277 us (63%)
  other arithmetic  96.8 us (22%)
  matrix products  23.4 us (5%)
  local copies, waits for them, and re-layouts  15.9 us (4%)
  between operations  14 us (3%)
  starting transfers between devices  10.6 us (2%)
    all_gather x1, waiting for transfers between devices, per_device(): gathered = lax.all_gather(hidden_states, 'head', axis=1, tiled=True)  107 us
    all_gather x1, waiting for transfers between devices, per_device(): lax.all_gather(key_projection_weight, ('seq', 'sub'), axis=0, tiled=True)  83.7 us
    all_gather x1, waiting for transfers between devices, per_device(): lax.all_gather(value_projection_weight, ('seq', 'sub'), axis=0, tiled=True)  52.6 us
    another operation x4, other arithmetic, per_device(): factor = jnp.linalg.cholesky(regular)  47.1 us
    another operation x3, other arithmetic, per_device(): lax.linalg.triangular_solve(factor, by_head, left_side=False, lower=True,...  39.4 us
    all_gather x1, waiting for transfers between devices, covariance_sum(): summed = jnp.sum(lax.all_gather(local_terms, ('seq', 'sub')), axis=0)  23.4 us
    dot_general x1, matrix products, per_device(): jnp.dot(gathered, lax.all_gather(key_projection_weight, ('seq', 'sub'), a...  10.3 us
    dot_general x1, matrix products, per_device(): jnp.dot(gathered, lax.all_gather(value_projection_weight, ('seq', 'sub'),...  10.2 us
  transfers between devices with their start and end apart: 7, of which 6 were waited for; matrix products, arithmetic and copies ran while one was open for 30% of the time, Pallas kernels for 0%

profile of v1, /device:TPU:0, one launch (start us, length us, event | category | flops | bytes accessed | tf_op | source)
XLA Modules:
  0.0 437.8 jit_solution(368886773795501532)
XLA Ops:
  7.2 0.7 all-gather.6.cloned.1.call-update
  8.0 0.7 all-gather.8.cloned.1.call-update
  8.7 0.7 all-gather.10.cloned.1.call-update
  9.5 106.8 %all-gather.6.cloned.1.call-done = bf16[512,8192]{1,0:T(8,128)(2,1)} async-done(((bf16[512,4096]{1,0:T(8,128)(2,1)}), bf16[512,8192]{1,0:T(8,128)(2,1)}) %all-gather.6.cloned.1.call-update) | async-done | bytes 8388624 | tf_op jit(solution)/shard_map/all_gather | solution.py:29
  116.3 83.7 %all-gather.8.cloned.1.call-done = bf16[8192,512]{1,0:T(8,128)(2,1)} async-done(((bf16[1024,512]{1,0:T(8,128)(2,1)}), bf16[8192,512]{1,0:T(8,128)(2,1)}) %all-gather.8.cloned.1.call-update) | async-done | bytes 8388624 | tf_op jit(solution)/shard_map/all_gather | solution.py:32
  200.0 10.3 %convolution_convert_fusion.1 = bf16[512,512]{0,1:T(8,128)(2,1)S(1)} fusion(bf16[512,8192]{1,0:T(8,128)(2,1)} %all-gather.6.cloned.1.call-done, bf16[8192,512]{1,0:T(8,128)(2,1)} %all-gather.8.cloned.1.call-done), kind=kOutput, calls=%fused_computation.6 | convolution fusion | flops 4295229440 | bytes 17301504 | tf_op jit(solution)/shard_map/dot_general | solution.py:30
  210.3 1.0 fusion.8
  211.3 3.8 sort.31
  215.1 3.5 gather_fusion
  218.6 0.7 all_to_all.24
  219.3 3.3 all-to-all-start
  222.8 5.3 %all-to-all-done = s32[8,64,1]{1,2,0:T(1,128)S(1)} async-done(((s32[8,64,1]{1,2,0:T(1,128)}), s32[8,64,1]{1,2,0:T(1,128)S(1)}, u32[]{:S(2)}, u32[]{:S(2)}) %all-to-all-start) | async-done | bytes 2080 | tf_op jit(solution)/shard_map/all_to_all | solution.py:63
  228.1 0.5 broadcast.149
  228.6 0.7 reduce.9
  229.4 0.3 copy.25
  229.7 52.6 %all-gather.10.cloned.1.call-done = bf16[8192,512]{1,0:T(8,128)(2,1)} async-done(((bf16[1024,512]{1,0:T(8,128)(2,1)}), bf16[8192,512]{1,0:T(8,128)(2,1)}) %all-gather.10.cloned.1.call-update) | async-done | bytes 8388624 | tf_op jit(solution)/shard_map/all_gather | solution.py:37
  282.3 10.2 %convolution_convert_fusion = bf16[512,512]{1,0:T(8,128)(2,1)S(1)} fusion(bf16[512,8192]{1,0:T(8,128)(2,1)} %all-gather.6.cloned.1.call-done, bf16[8192,512]{1,0:T(8,128)(2,1)} %all-gather.10.cloned.1.call-done), kind=kOutput, calls=%fused_computation.5 | convolution fusion | flops 4295229440 | bytes 17301504 | tf_op jit(solution)/shard_map/dot_general | solution.py:35
  292.5 2.6 gather_fusion.3
  295.2 3.7 all-to-all-start.2
  298.9 23.4 %all-gather.12.cloned.1.call-done = f32[32,128,128]{2,1,0:T(8,128)} async-done(((f32[4,128,128]{2,1,0:T(8,128)}), f32[32,128,128]{2,1,0:T(8,128)}) %all-gather.12.cloned.1.call-update) | async-done | bytes 2097168 | tf_op jit(solution)/shard_map/all_gather | solution.py:14
  322.3 1.7 reduce_sum.19
  324.5 46.9 %custom-call.7 = f32[4,128,128]{2,1,0:T(8,128)S(1)} custom-call(f32[4,128,128]{2,1,0:T(8,128)S(1)} %copy.29), custom_call_target="Cholesky" | custom-call | tf_op jit(solution)/shard_map/jit(cholesky)/cholesky | solution.py:46
  371.7 39.3 %custom-call.8 = f32[4,1,128,128]{2,3,1,0:T(8,128)S(1)} custom-call(f32[4,1,128,128]{3,2,1,0:T(8,128)S(1)} %select_bitcast_fusion), custom_call_target="InvertDiagBlocksLowerTriangular" | custom-call | tf_op jit(solution)/shard_map/triangular_solve | solution.py:50
  411.0 0.6 fusion
  411.6 1.3 convolution_convert_fusion.2
  412.9 0.1 copy.32
  413.0 2.6 gather_fusion.1
  415.6 3.4 all-to-all-start.1
  419.0 3.8 sort.32
  422.8 2.6 gather_fusion.4
  425.4 3.2 all-to-all-done.1
  428.7 2.6 gather_fusion.2
  (32 shorter events, 1.2 us)
Async XLA Ops:
  7.2 404.5 %copy-start = (f32[4,128,64]{1,2,0:T(8,128)S(1)}, f32[4,128,64]{1,2,0:T(8,128)}, u32[]{:S(2)}) copy-start(f32[4,128,64]{1,2,0:T(8,128)} %param.8) | copy-start | bytes 393220
  7.2 109.1 %all-gather.6.cloned.1.call-start = ((), (), s32[]{:S(2)}) async-start(), calls=%async_computation.3 | async-start | bytes 12582912 | tf_op jit(solution)/shard_map/all_gather | solution.py:29
  7.9 192.1 %all-gather.8.cloned.1.call-start = ((), (), s32[]{:S(2)}) async-start(), calls=%async_computation.4 | async-start | bytes 9437184 | tf_op jit(solution)/shard_map/all_gather | solution.py:32
  8.7 273.6 %all-gather.10.cloned.1.call-start = ((), (), s32[]{:S(2)}) async-start(), calls=%async_computation.5 | async-start | bytes 9437184 | tf_op jit(solution)/shard_map/all_gather | solution.py:37
  9.4 201.9 %copy-start.1 = (s32[512]{0:T(512)S(1)}, s32[512]{0:T(512)}, u32[]{:S(2)}) copy-start(s32[512]{0:T(512)} %param.9) | copy-start | bytes 6148
  9.4 312.9 %all-gather.12.cloned.1.call-start = ((), (), s32[]{:S(2)}) async-start(), calls=%async_computation.6 | async-start | bytes 2359296 | tf_op jit(solution)/shard_map/all_gather | solution.py:14
  219.3 8.8 %all-to-all-start = ((s32[8,64,1]{1,2,0:T(1,128)}), s32[8,64,1]{1,2,0:T(1,128)S(1)}, u32[]{:S(2)}, u32[]{:S(2)}) async-start(s32[8,64,1]{1,2,0:T(1,128)} %bitcast.8), calls=%async_computation | async-start | bytes 8192 | tf_op jit(solution)/shard_map/all_to_all | solution.py:63
  295.2 120.4 %all-to-all-start.2 = ((bf16[8,64,512]{2,1,0:T(8,128)(2,1)}), bf16[8,64,512]{2,1,0:T(8,128)(2,1)S(1)}, u32[]{:S(2)}, u32[]{:S(2)}) async-start(bf16[8,64,512]{2,1,0:T(8,128)(2,1)} %bitcast.12), calls=%async_computation.2 | async-start | bytes 1048576 | tf_op jit(solution)/shard_map/all_to_all | solution.py:69
  415.6 13.1 %all-to-all-start.1 = ((bf16[8,64,256]{2,1,0:T(8,128)(2,1)}), bf16[8,64,256]{2,1,0:T(8,128)(2,1)S(1)}, u32[]{:S(2)}, u32[]{:S(2)}) async-start(bf16[8,64,256]{2,1,0:T(8,128)(2,1)} %bitcast.10), calls=%async_computation.1 | async-start | bytes 524288 | tf_op jit(solution)/shard_map/all_to_all | solution.py:66
Sparse Core Ops, SparseCore 0:
  9.6 106.6 all-gather.5
  117.9 82.0 all-gather.7
  201.6 80.6 all-gather.9
  284.3 37.9 all-gather.11
